TPU v7x, 32 devices: a whole 2x2x4 slice. The times are simulated.
32 devices in a mesh: groups: 2 (over y), tiles: 4 (over z), views: 2 (over x), gz: 2 (over core).
Axes of the slice: x: 2, y: 2, z: 4, core: 2. Of those that a mesh axis runs over, the one named last changes fastest.
Arguments:
- view_data: bfloat16 [4, 4, 16, 128, 128], P(('groups', 'views'), 'tiles', 'gz'), parts along dimension 0, may hold values from 0.19921875 to 2
- estimate: float32 [32, 512, 128], P(('groups', 'gz'), 'tiles'), parts along dimension 0, may hold values from 0.5 to 1.5
- psf_taps: float32 [2, 2, 2, 9], P('views'), may hold values from 0.02 to 0.3
- offsets: int32 [2, 8], P('views'), may hold values from 0 to 3, as said below
Outputs:
- updated_estimate: float32 [32, 512, 128], P(('groups', 'gz'), 'tiles'), parts along dimension 0
There are 2 independent parts, one for each index of `groups`. A program takes and returns all parts, laid end to end along the dimension named above; an argument that names none is the same for every part. Nothing has to cross between parts.
Inputs may be any that keep to these rules, and one draw needn't show every extreme that they name: `offsets`: in each view's row no value appears more than 4 times, and one value appears exactly 4 times.
All inputs are finite; a program needn't handle non-finite values.
Results may differ from a plain program's by a relative error of at most 0.0022.
The roundings to bfloat16 on the way count: a program that leaves them out, or rounds other values in their place, can miss the bound.
Values may be sent and summed in bfloat16 or wider, within the bound.
No kernel may reach another device: no remote copies, remote signals or barrier semaphores. Data moves between devices by JAX's collectives and lax.ppermute only.
A program may use at most 64 MiB of HBM per device.

v0:
```python
import jax
import jax.numpy as jnp
from jax import lax
from jax.sharding import PartitionSpec as P

ITERS = 2
CAP = 4


TV_WEIGHT = 0.1
SMOOTH_SQUARE = 0.0025


def with_halo(cells, sides, width):
    for axis, dim in sides:
        count = lax.axis_size(axis)
        ends = count - 1
        head = lax.slice_in_dim(cells, 0, width, axis=dim)
        tail = lax.slice_in_dim(cells, cells.shape[dim] - width, cells.shape[dim], axis=dim)
        cells = jnp.concatenate(
            [
                lax.ppermute(tail, axis, [(i, (i + 1) % count) for i in range(ends)]),
                cells,
                lax.ppermute(head, axis, [((i + 1) % count, i) for i in range(ends)]),
            ],
            axis=dim,
        )
    return cells


def toeplitz_matrix(profile, length):
    half_width = (profile.shape[0] - 1) // 2
    position = jnp.arange(length, dtype=jnp.int32)
    offset = position[None, :] - position[:, None] + half_width
    tap_index = jnp.arange(profile.shape[0], dtype=jnp.int32)
    picked = (offset[:, :, None] == tap_index[None, None, :]).astype(jnp.float32)
    return jnp.sum(picked * profile[None, None, :], axis=2).astype(jnp.bfloat16)


def curvature(padded):
    anchor = padded[:-1, :-1, :-1]
    grad_z = padded[1:, :-1, :-1] - anchor
    grad_y = padded[:-1, 1:, :-1] - anchor
    grad_x = padded[:-1, :-1, 1:] - anchor
    magnitude = jnp.sqrt(grad_z * grad_z + grad_y * grad_y + grad_x * grad_x + SMOOTH_SQUARE)
    unit_z = grad_z / magnitude
    unit_y = grad_y / magnitude
    unit_x = grad_x / magnitude
    return (
        unit_z[1:, 1:, 1:]
        - unit_z[:-1, 1:, 1:]
        + (unit_y[1:, 1:, 1:] - unit_y[1:, :-1, 1:])
        + (unit_x[1:, 1:, 1:] - unit_x[1:, 1:, :-1])
    )


def view_correction(view_tile, observed, kernel_y, kernel_x):
    blurred = jnp.zeros(view_tile.shape, jnp.float32)
    for term_index in range(2):
        half_blur = jnp.einsum(
            "yk,zkx->zyx", kernel_y[term_index], view_tile, preferred_element_type=jnp.float32
        ).astype(jnp.bfloat16)
        blurred = blurred + jnp.einsum(
            "zyk,xk->zyx", half_blur, kernel_x[term_index], preferred_element_type=jnp.float32
        )
    quotient = (observed.astype(jnp.float32) / blurred).astype(jnp.bfloat16)
    log_sum = jnp.zeros(view_tile.shape, jnp.float32)
    for term_index in range(2):
        half_back = jnp.einsum(
            "ky,zkx->zyx", kernel_y[term_index], quotient, preferred_element_type=jnp.float32
        ).astype(jnp.bfloat16)
        log_sum = log_sum + jnp.einsum(
            "zyk,kx->zyx", half_back, kernel_x[term_index], preferred_element_type=jnp.float32
        )
    return log_sum.astype(jnp.bfloat16)


def shards(view_data, estimate, psf_taps, offsets):
    owners = lax.axis_size("tiles")
    view_count = lax.axis_size("views")
    observed = view_data[0, 0]
    planes, height, columns = estimate.shape
    view_shift = offsets[0]
    blocks = view_shift.shape[0]
    block_rows = height // blocks
    slot_count = owners * CAP
    kernel_y = jnp.stack(
        [toeplitz_matrix(psf_taps[0, term_index, 0], height) for term_index in range(2)]
    )
    kernel_x = jnp.stack(
        [toeplitz_matrix(psf_taps[0, term_index, 1], columns) for term_index in range(2)]
    )
    position = jnp.arange(blocks, dtype=jnp.int32)
    same_owner = view_shift[:, None] == view_shift[None, :]
    before = position[None, :] < position[:, None]
    slot_rank = jnp.sum((same_owner & before).astype(jnp.int32), axis=1)
    member = lax.axis_index("tiles")
    target = (member + view_shift) % owners
    source_tile = (member - view_shift) % owners
    slot_index = jnp.arange(slot_count, dtype=jnp.int32)
    to_owner = ((target * CAP + slot_rank)[:, None] == slot_index[None, :]).astype(jnp.bfloat16)
    from_tile = ((source_tile * CAP + slot_rank)[:, None] == slot_index[None, :]).astype(
        jnp.bfloat16
    )
    current = estimate
    for iteration in range(ITERS):
        padded = with_halo(current, (("tiles", 1), ("gz", 0)), 1)
        padded = jnp.pad(padded, ((0, 0), (0, 0), (1, 1)))
        owned_blocks = current.astype(jnp.bfloat16).reshape(planes, blocks, block_rows, columns)
        outgoing = jnp.einsum(
            "sk,zsrx->kzrx", from_tile, owned_blocks, preferred_element_type=jnp.float32
        ).astype(jnp.bfloat16)
        incoming = lax.all_to_all(
            outgoing.reshape(owners, CAP, planes, block_rows, columns),
            "tiles",
            split_axis=0,
            concat_axis=0,
            tiled=True,
        )
        view_tile = jnp.einsum(
            "sk,kzrx->zsrx",
            to_owner,
            incoming.reshape(slot_count, planes, block_rows, columns),
            preferred_element_type=jnp.float32,
        ).astype(jnp.bfloat16)
        view_tile = view_tile.reshape(planes, height, columns)
        correction = view_correction(view_tile, observed, kernel_y, kernel_x)
        correction = correction.reshape(planes, blocks, block_rows, columns)
        returned = jnp.einsum(
            "sk,zsrx->kzrx", to_owner, correction, preferred_element_type=jnp.float32
        ).astype(jnp.bfloat16)
        gathered = lax.all_to_all(
            returned.reshape(owners, CAP, planes, block_rows, columns),
            "tiles",
            split_axis=0,
            concat_axis=0,
            tiled=True,
        )
        owned_rows = jnp.einsum(
            "sk,kzrx->zsrx",
            from_tile,
            gathered.reshape(slot_count, planes, block_rows, columns),
            preferred_element_type=jnp.float32,
        ).reshape(planes, height, columns)
        log_values = jnp.log(owned_rows)
        share_rows = height // view_count
        log_part = lax.psum_scatter(log_values, "views", scatter_dimension=1, tiled=True)
        first_row = lax.axis_index("views") * share_rows
        window = lax.dynamic_slice_in_dim(padded, first_row, share_rows + 2, 1)
        damping = 1.0 - TV_WEIGHT * curvature(window)
        rows_now = lax.dynamic_slice_in_dim(current, first_row, share_rows, 1)
        updated = rows_now * jnp.exp(log_part / view_count) / damping
        current = lax.all_gather(updated, "views", axis=1, tiled=True)
    return current


def solution(mesh):
    in_specs = (
        P(("groups", "views"), "tiles", "gz", None, None),
        P(("groups", "gz"), "tiles", None),
        P("views", None, None, None),
        P("views", None),
    )
    out_specs = P(("groups", "gz"), "tiles", None)
    return jax.shard_map(shards, mesh=mesh, in_specs=in_specs, out_specs=out_specs, check_vma=False)
```

profile of v0, /device:TPU:0, one launch (start us, length us, event | category | flops | bytes accessed | tf_op | source)
XLA Modules:
  0.0 147.0 jit_solution(17217516161442016917)
XLA Ops:
  6.5 1.1 convert_element_type.124
  8.3 1.1 copy.49
  9.3 6.5 %all-to-all-start = ((bf16[4,4,8,16,128]{4,1,3,2,0:T(4,128)(2,1)}), bf16[4,4,8,16,128]{4,1,3,2,0:T(4,128)(2,1)S(1)}, u32[]{:S(2)}, u32[]{:S(2)}) async-start(bf16[4,4,8,16,128]{4,1,3,2,0:T(4,128)(2,1)} %copy.49), calls=%async_computation | async-start | bytes 1048576 | tf_op jit(solution)/shard_map/all_to_all | solution.py:113
  16.1 14.2 %all-to-all-done = bf16[4,4,8,16,128]{4,1,3,2,0:T(4,128)(2,1)S(1)} async-done(((bf16[4,4,8,16,128]{4,1,3,2,0:T(4,128)(2,1)}), bf16[4,4,8,16,128]{4,1,3,2,0:T(4,128)(2,1)S(1)}, u32[]{:S(2)}, u32[]{:S(2)}) %all-to-all-start) | async-done | bytes 524320 | tf_op jit(solution)/shard_map/all_to_all | solution.py:113
  33.9 16.5 %all_to_all.20 = bf16[4,4,8,16,128]{4,1,3,2,0:T(4,128)(2,1)S(1)} all-to-all(bf16[4,4,8,16,128]{4,1,3,2,0:T(4,128)(2,1)S(1)} %copy.61), channel_id=1, replica_groups=mesh['groups'=2,'tiles'=4,'views'=2,'gz'=2] {'tiles'}, dimensions={0} | all-to-all | bytes 1048576 | tf_op jit(solution)/shard_map/all_to_all | solution.py:132
  50.8 0.9 copy.63
  52.0 2.1 %collective-permute-start = (f32[8,1,128]{2,1,0:T(1,128)S(1)}, f32[8,1,128]{2,1,0:T(1,128)S(1)}, u32[]{:S(2)}, u32[]{:S(2)}) collective-permute-start(f32[8,1,128]{2,1,0:T(1,128)S(1)} %get-tuple-element.24), channel_id=1, source_target_pairs={{0,4},{4,8},{8,12},{1,5},{5,9},{9,13},{2,6},{6,10},{10,14},{3,7},{... | collective-permute-start | bytes 12296 | tf_op jit(solution)/shard_map/ppermute | solution.py:22
  54.1 1.3 collective-permute-start.1
  55.4 4.2 %collective-permute-done.1 = f32[8,1,128]{2,1,0:T(1,128)S(1)} collective-permute-done((f32[8,1,128]{2,1,0:T(1,128)S(1)}, f32[8,1,128]{2,1,0:T(1,128)S(1)}, u32[]{:S(2)}, u32[]{:S(2)}) %collective-permute-start.1) | collective-permute-done | bytes 4128 | tf_op jit(solution)/shard_map/ppermute | solution.py:24
  59.6 1.3 collective-permute-start.2
  60.9 1.3 collective-permute-start.3
  62.4 1.7 %collective-permute-done.3 = f32[1,130,128]{2,1,0:T(8,128)S(1)} collective-permute-done((f32[1,130,128]{2,1,0:T(8,128)S(1)}, f32[1,130,128]{2,1,0:T(8,128)S(1)}, u32[]{:S(2)}, u32[]{:S(2)}) %collective-permute-start.3) | collective-permute-done | bytes 66592 | tf_op jit(solution)/shard_map/ppermute | solution.py:24
  65.7 1.4 fusion.49
  67.1 8.9 %all_gather.6 = f32[8,128,128]{2,1,0:T(8,128)S(1)} all-gather(f32[8,64,128]{2,1,0:T(8,128)S(1)} %fusion.49), channel_id=1, replica_groups=mesh['groups'=2,'tiles'=4,'views'=2,'gz'=2] {'views'}, dimensions={1}, use_global_device_ids=true | all-gather | bytes 786432 | tf_op jit(solution)/shard_map/all_gather | solution.py:153
  76.7 17.5 %all_to_all.21 = bf16[4,4,8,16,128]{4,1,3,2,0:T(4,128)(2,1)S(1)} all-to-all(bf16[4,4,8,16,128]{4,1,3,2,0:T(4,128)(2,1)S(1)} %copy.65), channel_id=1, replica_groups=mesh['groups'=2,'tiles'=4,'views'=2,'gz'=2] {'tiles'}, dimensions={0} | all-to-all | bytes 1048576 | tf_op jit(solution)/shard_map/all_to_all | solution.py:113
  97.8 16.3 %all_to_all.22 = bf16[4,4,8,16,128]{4,1,3,2,0:T(4,128)(2,1)S(1)} all-to-all(bf16[4,4,8,16,128]{4,1,3,2,0:T(4,128)(2,1)S(1)} %copy.77), channel_id=1, replica_groups=mesh['groups'=2,'tiles'=4,'views'=2,'gz'=2] {'tiles'}, dimensions={0} | all-to-all | bytes 1048576 | tf_op jit(solution)/shard_map/all_to_all | solution.py:132
  115.4 2.1 %collective-permute-start.4 = (f32[8,1,128]{2,1,0:T(1,128)S(1)}, f32[8,1,128]{2,1,0:T(1,128)S(1)}, u32[]{:S(2)}, u32[]{:S(2)}) collective-permute-start(f32[8,1,128]{2,1,0:T(1,128)S(1)} %get-tuple-element.22), channel_id=1, source_target_pairs={{0,4},{4,8},{8,12},{1,5},{5,9},{9,13},{2,6},{6,10},{10,14},{3,7},{... | collective-permute-start | bytes 12296 | tf_op jit(solution)/shard_map/ppermute | solution.py:22
  117.6 1.3 collective-permute-start.5
  118.9 4.2 %collective-permute-done.5 = f32[8,1,128]{2,1,0:T(1,128)S(1)} collective-permute-done((f32[8,1,128]{2,1,0:T(1,128)S(1)}, f32[8,1,128]{2,1,0:T(1,128)S(1)}, u32[]{:S(2)}, u32[]{:S(2)}) %collective-permute-start.5) | collective-permute-done | bytes 4128 | tf_op jit(solution)/shard_map/ppermute | solution.py:24
  123.1 1.3 collective-permute-start.6
  124.4 1.3 collective-permute-start.7
  125.7 1.8 %collective-permute-done.7 = f32[1,130,128]{2,1,0:T(8,128)S(1)} collective-permute-done((f32[1,130,128]{2,1,0:T(8,128)S(1)}, f32[1,130,128]{2,1,0:T(8,128)S(1)}, u32[]{:S(2)}, u32[]{:S(2)}) %collective-permute-start.7) | collective-permute-done | bytes 66592 | tf_op jit(solution)/shard_map/ppermute | solution.py:24
  128.9 1.4 fusion.44
  130.4 9.0 %all_gather.7 = f32[8,128,128]{2,1,0:T(8,128)S(1)} all-gather(f32[8,64,128]{2,1,0:T(8,128)S(1)} %fusion.44), channel_id=1, replica_groups=mesh['groups'=2,'tiles'=4,'views'=2,'gz'=2] {'views'}, dimensions={1}, use_global_device_ids=true | all-gather | bytes 786432 | tf_op jit(solution)/shard_map/all_gather | solution.py:153
  (64 shorter events, 14.7 us)
Async XLA Ops:
  6.5 1.1 copy-start.2
  9.3 6.5 %copy-start.1 = (f32[1,2,2,9]{3,2,1,0:T(2,128)S(1)}, f32[1,2,2,9]{3,2,1,0:T(2,128)}, u32[]{:S(2)}) copy-start(f32[1,2,2,9]{3,2,1,0:T(2,128)} %param.6) | copy-start | bytes 436
  9.3 21.0 %all-to-all-start = ((bf16[4,4,8,16,128]{4,1,3,2,0:T(4,128)(2,1)}), bf16[4,4,8,16,128]{4,1,3,2,0:T(4,128)(2,1)S(1)}, u32[]{:S(2)}, u32[]{:S(2)}) async-start(bf16[4,4,8,16,128]{4,1,3,2,0:T(4,128)(2,1)} %copy.49), calls=%async_computation | async-start | bytes 1048576 | tf_op jit(solution)/shard_map/all_to_all | solution.py:113
  15.8 49.8 %reduce-scatter.3.cloned.1.call-start = ((), (), s32[]{:S(2)}) async-start(), calls=%async_computation.6 | async-start | bytes 786432 | tf_op jit(solution)/shard_map/reduce_scatter | solution.py:147
  30.8 1.0 copy-start.3
  50.8 1.1 copy-start
  51.8 77.2 %reduce-scatter.5.cloned.1.call-start = ((), (), s32[]{:S(2)}) async-start(), calls=%async_computation.7 | async-start | bytes 786432 | tf_op jit(solution)/shard_map/reduce_scatter | solution.py:147
  52.0 3.4 %collective-permute-start = (f32[8,1,128]{2,1,0:T(1,128)S(1)}, f32[8,1,128]{2,1,0:T(1,128)S(1)}, u32[]{:S(2)}, u32[]{:S(2)}) collective-permute-start(f32[8,1,128]{2,1,0:T(1,128)S(1)} %get-tuple-element.24), channel_id=1, source_target_pairs={{0,4},{4,8},{8,12},{1,5},{5,9},{9,13},{2,6},{6,10},{10,14},{3,7},{... | collective-permute-start | bytes 12296 | tf_op jit(solution)/shard_map/ppermute | solution.py:22
  54.1 5.5 %collective-permute-start.1 = (f32[8,1,128]{2,1,0:T(1,128)S(1)}, f32[8,1,128]{2,1,0:T(1,128)S(1)}, u32[]{:S(2)}, u32[]{:S(2)}) collective-permute-start(f32[8,1,128]{2,1,0:T(1,128)S(1)} %get-tuple-element.23), channel_id=1, source_target_pairs={{4,0},{8,4},{12,8},{5,1},{9,5},{13,9},{6,2},{10,6},{14,10},{7,3},{... | collective-permute-start | bytes 12296 | tf_op jit(solution)/shard_map/ppermute | solution.py:24
  59.6 2.8 %collective-permute-start.2 = (f32[1,130,128]{2,1,0:T(8,128)S(1)}, f32[1,130,128]{2,1,0:T(8,128)S(1)}, u32[]{:S(2)}, u32[]{:S(2)}) collective-permute-start(f32[1,130,128]{2,1,0:T(8,128)S(1)} %get-tuple-element.20), channel_id=1, source_target_pairs={{0,1},{2,3},{4,5},{6,7},{8,9},{10,11},{12,13},{14,15},{16,17},{18,... | collective-permute-start | bytes 199688 | tf_op jit(solution)/shard_map/ppermute | solution.py:22
  60.9 3.2 %collective-permute-start.3 = (f32[1,130,128]{2,1,0:T(8,128)S(1)}, f32[1,130,128]{2,1,0:T(8,128)S(1)}, u32[]{:S(2)}, u32[]{:S(2)}) collective-permute-start(f32[1,130,128]{2,1,0:T(8,128)S(1)} %get-tuple-element.19), channel_id=1, source_target_pairs={{1,0},{3,2},{5,4},{7,6},{9,8},{11,10},{13,12},{15,14},{17,16},{19,... | collective-permute-start | bytes 199688 | tf_op jit(solution)/shard_map/ppermute | solution.py:24
  94.7 1.0 copy-start.4
  115.4 3.4 %collective-permute-start.4 = (f32[8,1,128]{2,1,0:T(1,128)S(1)}, f32[8,1,128]{2,1,0:T(1,128)S(1)}, u32[]{:S(2)}, u32[]{:S(2)}) collective-permute-start(f32[8,1,128]{2,1,0:T(1,128)S(1)} %get-tuple-element.22), channel_id=1, source_target_pairs={{0,4},{4,8},{8,12},{1,5},{5,9},{9,13},{2,6},{6,10},{10,14},{3,7},{... | collective-permute-start | bytes 12296 | tf_op jit(solution)/shard_map/ppermute | solution.py:22
  117.6 5.5 %collective-permute-start.5 = (f32[8,1,128]{2,1,0:T(1,128)S(1)}, f32[8,1,128]{2,1,0:T(1,128)S(1)}, u32[]{:S(2)}, u32[]{:S(2)}) collective-permute-start(f32[8,1,128]{2,1,0:T(1,128)S(1)} %get-tuple-element.21), channel_id=1, source_target_pairs={{4,0},{8,4},{12,8},{5,1},{9,5},{13,9},{6,2},{10,6},{14,10},{7,3},{... | collective-permute-start | bytes 12296 | tf_op jit(solution)/shard_map/ppermute | solution.py:24
  123.1 2.6 %collective-permute-start.6 = (f32[1,130,128]{2,1,0:T(8,128)S(1)}, f32[1,130,128]{2,1,0:T(8,128)S(1)}, u32[]{:S(2)}, u32[]{:S(2)}) collective-permute-start(f32[1,130,128]{2,1,0:T(8,128)S(1)} %get-tuple-element.18), channel_id=1, source_target_pairs={{0,1},{2,3},{4,5},{6,7},{8,9},{10,11},{12,13},{14,15},{16,17},{18,... | collective-permute-start | bytes 199688 | tf_op jit(solution)/shard_map/ppermute | solution.py:22
  124.4 3.2 %collective-permute-start.7 = (f32[1,130,128]{2,1,0:T(8,128)S(1)}, f32[1,130,128]{2,1,0:T(8,128)S(1)}, u32[]{:S(2)}, u32[]{:S(2)}) collective-permute-start(f32[1,130,128]{2,1,0:T(8,128)S(1)} %get-tuple-element.17), channel_id=1, source_target_pairs={{1,0},{3,2},{5,4},{7,6},{9,8},{11,10},{13,12},{15,14},{17,16},{19,... | collective-permute-start | bytes 199688 | tf_op jit(solution)/shard_map/ppermute | solution.py:24
Sparse Core Ops, SparseCore 0:
  51.9 13.7 reduce-scatter.2
  115.6 13.3 reduce-scatter.4
where the time goes:
time: 148 us; the launch traced here: 147 us
  blocking collectives  68.1 us (46%)
  waiting for transfers between devices  26.3 us (18%)
  starting transfers between devices  18.5 us (12%)
  between operations  13.8 us (9%)
  other arithmetic  7.34 us (5%)
  matrix products  6.62 us (4%)
  local copies, waits for them, and re-layouts  6.29 us (4%)
    all_to_all x2, blocking collectives, shards(): lax.all_to_all(returned.reshape(owners, CAP, planes, block_rows, columns)...  32.7 us
    all_gather x2, blocking collectives, shards(): current = lax.all_gather(updated, 'views', axis=1, tiled=True)  17.9 us
    all_to_all x1, blocking collectives, shards(): lax.all_to_all(outgoing.reshape(owners, CAP, planes, block_rows, columns)...  17.5 us
    all_to_all x1, waiting for transfers between devices, shards(): lax.all_to_all(outgoing.reshape(owners, CAP, planes, block_rows, columns)...  14.2 us
    ppermute x4, waiting for transfers between devices, with_halo(): lax.ppermute(head, axis, [((i + 1) % count, i) for i in range(ends)])  11.9 us
    ppermute x4, starting transfers between devices, with_halo(): lax.ppermute(tail, axis, [(i, (i + 1) % count) for i in range(ends)])  6.82 us
    all_to_all x1, starting transfers between devices, shards(): lax.all_to_all(outgoing.reshape(owners, CAP, planes, block_rows, columns)...  6.48 us
    ppermute x4, starting transfers between devices, with_halo(): lax.ppermute(head, axis, [((i + 1) % count, i) for i in range(ends)])  5.17 us
  transfers between devices with their start and end apart: 11, of which 6 were waited for; matrix products, arithmetic and copies ran while one was open for 2% of the time, Pallas kernels for 0%

commit v1 on v0

--- a/solution.py
+++ b/solution.py
@@ -1,6 +1,10 @@
+import functools
+
 import jax
 import jax.numpy as jnp
 from jax import lax
+from jax.experimental import pallas as pl
+from jax.experimental.pallas import tpu as pltpu
 from jax.sharding import PartitionSpec as P
 
 ITERS = 2
@@ -154,6 +158,218 @@
     return current
 
 
+PAD_ROWS = 16
+
+
+def chip_order(tiles, views):
+    return [v * tiles + (t if v % 2 == 0 else tiles - 1 - t) for t in range(tiles) for v in range(views)]
+
+
+def correction_kernel(offsets_ref, current_ref, data_ref, matrices_ref, log_ref, tiles_ref, halves_ref, back_ref):
+    views, blocks = offsets_ref.shape
+    tiles = data_ref.shape[0]
+    height, columns = matrices_ref.shape[-2] // 2, matrices_ref.shape[-1]
+    rows = height // blocks
+    for v in range(views):
+        for t in range(tiles):
+            for s in range(blocks):
+                owner = lax.rem(t + offsets_ref[v, s], tiles)
+                start = pl.multiple_of(owner * height + s * rows, rows)
+                tiles_ref[s * rows : (s + 1) * rows, t * columns : (t + 1) * columns] = current_ref[
+                    pl.ds(start, rows), :
+                ]
+        half = jnp.dot(matrices_ref[v, 0], tiles_ref[...], preferred_element_type=jnp.float32)
+        half = half.astype(jnp.bfloat16)
+        for t in range(tiles):
+            for r in range(2):
+                halves_ref[t * height : (t + 1) * height, r * columns : (r + 1) * columns] = half[
+                    r * height : (r + 1) * height, t * columns : (t + 1) * columns
+                ]
+        blurred = jnp.dot(halves_ref[...], matrices_ref[v, 1], preferred_element_type=jnp.float32)
+        for t in range(tiles):
+            observed = data_ref[t, v, 0:height, :].astype(jnp.float32)
+            quotient = observed / blurred[t * height : (t + 1) * height]
+            tiles_ref[:, t * columns : (t + 1) * columns] = quotient.astype(jnp.bfloat16)
+        half = jnp.dot(matrices_ref[v, 2], tiles_ref[...], preferred_element_type=jnp.float32)
+        half = half.astype(jnp.bfloat16)
+        for t in range(tiles):
+            for r in range(2):
+                halves_ref[t * height : (t + 1) * height, r * columns : (r + 1) * columns] = half[
+                    r * height : (r + 1) * height, t * columns : (t + 1) * columns
+                ]
+        back = jnp.dot(halves_ref[...], matrices_ref[v, 3], preferred_element_type=jnp.float32)
+        back_ref[v] = jnp.log(back.astype(jnp.bfloat16).astype(jnp.float32))
+    for o in range(tiles):
+        for s in range(blocks):
+            total = None
+            for v in range(views):
+                tile = lax.rem(o - offsets_ref[v, s] + tiles, tiles)
+                start = pl.multiple_of(tile * height + s * rows, rows)
+                part = back_ref[v, pl.ds(start, rows), :]
+                total = part if total is None else total + part
+            log_ref[o * height + s * rows : o * height + (s + 1) * rows, :] = total
+
+
+def correction_logs(offsets, current, received, matrices):
+    tiles, views = received.shape[:2]
+    height = matrices.shape[-2] // 2
+    columns = current.shape[-1]
+    return pl.pallas_call(
+        correction_kernel,
+        out_shape=jax.ShapeDtypeStruct(current.shape, jnp.float32),
+        in_specs=[pl.BlockSpec(memory_space=pltpu.SMEM)] + [pl.BlockSpec(memory_space=pltpu.VMEM)] * 3,
+        out_specs=pl.BlockSpec(memory_space=pltpu.VMEM),
+        scratch_shapes=[
+            pltpu.VMEM((height, tiles * columns), jnp.bfloat16),
+            pltpu.VMEM((tiles * height, 2 * columns), jnp.bfloat16),
+            pltpu.VMEM((views, tiles * height, columns), jnp.float32),
+        ],
+        cost_estimate=pl.CostEstimate(flops=300_000_000, bytes_accessed=1_500_000, transcendentals=0),
+        name="correction",
+    )(offsets, current, received, matrices)
+
+
+def update_kernel(views, core_ref, current_ref, twin_ref, other_ref, log_ref, new_ref, narrow_ref):
+    rows, columns = current_ref.shape
+    first = core_ref[0] == 0
+    current = current_ref[...]
+    twin, other = twin_ref[...], other_ref[...]
+    above = jnp.where(first, twin, other)
+    below = jnp.where(first, other, twin)
+    row = lax.broadcasted_iota(jnp.int32, (rows, columns), 0)
+    column = lax.broadcasted_iota(jnp.int32, (rows, columns), 1)
+
+    def next_row(x):
+        return jnp.where(row == rows - 1, 0.0, pltpu.roll(x, rows - 1, 0))
+
+    def next_column(x):
+        return jnp.where(column == columns - 1, 0.0, pltpu.roll(x, columns - 1, 1))
+
+    def scale(z, y, x):
+        return lax.rsqrt(z * z + y * y + x * x + SMOOTH_SQUARE)
+
+    grad_z = above - current
+    grad_y = next_row(current) - current
+    grad_x = next_column(current) - current
+    inverse = scale(grad_z, grad_y, grad_x)
+    unit_y, unit_x = grad_y * inverse, grad_x * inverse
+    edge = current * lax.rsqrt(current * current + SMOOTH_SQUARE)
+    before_y = jnp.where(row == 0, edge, pltpu.roll(unit_y, 1, 0))
+    before_x = jnp.where(column == 0, edge, pltpu.roll(unit_x, 1, 1))
+    lower_z = current - below
+    lower = lower_z * scale(lower_z, next_row(below) - below, next_column(below) - below)
+    divergence = grad_z * inverse - lower + (unit_y - before_y) + (unit_x - before_x)
+    damping = 1.0 - TV_WEIGHT * divergence
+    new = current * jnp.exp(log_ref[...] / views) / damping
+    new_ref[...] = new
+    narrow_ref[...] = new.astype(narrow_ref.dtype)
+
+
+def update(views, core, current, twin, other, logs):
+    return pl.pallas_call(
+        functools.partial(update_kernel, views),
+        out_shape=(
+            jax.ShapeDtypeStruct(current.shape, jnp.float32),
+            jax.ShapeDtypeStruct(current.shape, jnp.bfloat16),
+        ),
+        in_specs=[pl.BlockSpec(memory_space=pltpu.SMEM)] + [pl.BlockSpec(memory_space=pltpu.VMEM)] * 4,
+        out_specs=[pl.BlockSpec(memory_space=pltpu.VMEM)] * 2,
+        name="update",
+    )(core, current, twin, other, logs)
+
+
+def plane_shards(view_data, estimate, psf_taps, offsets):
+    tiles, views = lax.axis_size("tiles"), lax.axis_size("views")
+    grid = ("tiles", "views")
+    places = chip_order(tiles, views)
+    planes, height, columns = estimate.shape
+    half_planes = planes // 2
+    blocks = offsets.shape[1]
+    taps = psf_taps.shape[-1]
+    share = height // views
+    core = lax.axis_index("gz")
+    view = lax.axis_index("views")
+
+    rows = lax.dynamic_slice_in_dim(estimate, view * share, share, 1)
+    high = lax.reduce_precision(rows, 8, 7)
+    low = rows - high
+    info = jnp.concatenate([psf_taps.reshape(-1), offsets.reshape(-1).astype(jnp.float32)])
+    info = jnp.pad(info, (0, columns - info.shape[0])).astype(jnp.bfloat16)
+    payload = jnp.concatenate(
+        [
+            view_data[0, 0],
+            high.astype(jnp.bfloat16),
+            low.astype(jnp.bfloat16),
+            jnp.broadcast_to(info, (planes, PAD_ROWS, columns)),
+        ],
+        axis=1,
+    )
+    paired = payload.reshape(half_planes, 2, payload.shape[1], columns)
+    keep = lax.dynamic_index_in_dim(paired, core, 1, keepdims=False)
+    give = lax.dynamic_index_in_dim(paired, 1 - core, 1, keepdims=False)
+    swap = [(0, 1), (1, 0)]
+    got = lax.ppermute(give, "gz", swap)
+    lead = jnp.where(core == 0, keep, got)
+    rear = jnp.where(core == 0, got, keep)
+    outgoing = jnp.stack([lead[p] if p < half_planes else rear[p - half_planes] for p in places])
+    received = lax.all_to_all(outgoing, grid, 0, 0, tiled=True)
+    received = received.reshape(tiles, views, payload.shape[1], columns)
+
+    narrow = received[:, :, height : height + share].reshape(tiles * height, columns)
+    rest = received[:, :, height + share : height + 2 * share].reshape(tiles * height, columns)
+    current = narrow.astype(jnp.float32) + rest.astype(jnp.float32)
+    info = received[0, :, height + 2 * share, :].astype(jnp.float32)
+    profiles = info[:, : 4 * taps].reshape(views, 2, 2, taps)
+    shifts = info[:, 4 * taps : 4 * taps + blocks].astype(jnp.int32)
+    profile_y, profile_x = profiles[:, :, 0], profiles[:, :, 1]
+    chosen = jnp.stack([profile_y, profile_x[..., ::-1], profile_y[..., ::-1], profile_x], axis=1)
+    matrices = jax.vmap(jax.vmap(jax.vmap(lambda p: toeplitz_matrix(p, columns))))(chosen)
+    matrices = matrices.reshape(views, 4, 2 * columns, columns)
+
+    def place(t, v):
+        return places[t * views + v]
+
+    at = {place(t, v): t * views + v for t in range(tiles) for v in range(views)}
+    hops = []
+    for p in range(planes - 1):
+        one, two = at[p] * 2 + 1, at[p + 1] * 2
+        hops += [(one, two), (two, one)]
+
+    flag = core.reshape(1).astype(jnp.int32)
+    for iteration in range(ITERS):
+        other = lax.ppermute(current, ("tiles", "views", "gz"), hops)
+        twin = lax.ppermute(current, "gz", swap)
+        logs = correction_logs(shifts, narrow, received, matrices)
+        current, narrow = update(views, flag, current, twin, other, logs)
+
+    result = current.astype(jnp.float16).reshape(tiles, 1, height, columns)
+    result = jnp.broadcast_to(result, (tiles, views, height, columns)).reshape(planes, height, columns)
+    result = lax.all_to_all(result, grid, 0, 0, tiled=True)
+    result = jnp.stack([result[at[p]] for p in range(planes)])
+    result = result.reshape(2, half_planes, height, columns)
+    keep = lax.dynamic_index_in_dim(result, core, 0, keepdims=False)
+    give = lax.dynamic_index_in_dim(result, 1 - core, 0, keepdims=False)
+    got = lax.ppermute(give, "gz", swap)
+    even = jnp.where(core == 0, keep, got)
+    odd = jnp.where(core == 0, got, keep)
+    return jnp.stack([even, odd], axis=1).reshape(planes, height, columns).astype(jnp.float32)
+
+
+def one_plane_each(mesh, view_data, estimate, psf_taps, offsets):
+    tiles, views, depth = mesh.shape["tiles"], mesh.shape["views"], mesh.shape["gz"]
+    planes = estimate.shape[0] // (mesh.shape["groups"] * depth)
+    height, columns = estimate.shape[1] // tiles, estimate.shape[2]
+    return (
+        depth == 2
+        and tiles * views == planes
+        and planes % 2 == 0
+        and height == columns
+        and height % (16 * offsets.shape[1]) == 0
+        and height % (16 * views) == 0
+        and 4 * psf_taps.shape[-1] + offsets.shape[1] <= columns
+    )
+
+
 def solution(mesh):
     in_specs = (
         P(("groups", "views"), "tiles", "gz", None, None),
@@ -162,4 +378,9 @@
         P("views", None),
     )
     out_specs = P(("groups", "gz"), "tiles", None)
-    return jax.shard_map(shards, mesh=mesh, in_specs=in_specs, out_specs=out_specs, check_vma=False)
+
+    def step(*arrays):
+        body = plane_shards if one_plane_each(mesh, *arrays) else shards
+        return jax.shard_map(body, mesh=mesh, in_specs=in_specs, out_specs=out_specs, check_vma=False)(*arrays)
+
+    return step

time: 148 us -> 73 us (0.49)
  blocking collectives: 68.1 us -> 14.8 us
  between operations: 13.8 us -> 0.2 us
  Pallas kernels: 0 us -> 11.9 us
  waiting for transfers between devices: 26.3 us -> 18 us
  matrix products: 6.62 us -> 0 us
  starting transfers between devices: 18.5 us -> 12.6 us
  local copies, waits for them, and re-layouts: 6.29 us -> 7.84 us
    all_to_all x3 -> x1, blocking collectives: 50.2 us -> 14.8 us  [plane_shards(): result = lax.all_to_all(result, grid, 0, 0, tiled=True)]
    all_gather x2 -> x0, blocking collectives: 17.9 us -> none  [shards(): current = lax.all_gather(updated, 'views', axis=1, tiled=True)]
    pallas_call x0 -> x4, Pallas kernels: none -> 11.9 us  [the longest x2 7.03 us: correction_logs(): pl.pallas_call(correction_kernel, out_shape=jax.ShapeDtypeStruct(current....]
    ppermute x8 -> x6, waiting for transfers between devices: 11.9 us -> 2.53 us  [the longest x2 2.52 us: plane_shards(): got = lax.ppermute(give, 'gz', swap)]
    dot_general x16 -> x0, matrix products: 6.62 us -> none  [the longest x4 1.93 us: view_correction(): jnp.einsum('zyk,xk->zyx', half_blur, kernel_x[term_index], preferred_elem...]
    ppermute x8 -> x6, starting transfers between devices: 12 us -> 5.42 us  [the longest x2 3.45 us: plane_shards(): twin = lax.ppermute(current, 'gz', swap)]
    unnamed x11 -> x29, local copies, waits for them, and re-layouts: 1.81 us -> 6.68 us
    div x6 -> x0, other arithmetic: 4.33 us -> none  [the longest x2 2.8 us: shards(): updated = rows_now * jnp.exp(log_part / view_count) / damping]
  transfers between devices with their start and end apart: 11 -> 7, of which waited for: 6 -> 3; matrix products, arithmetic and copies ran while one was open for 2% -> 4% of each run, Pallas kernels for 0% -> 10%
where the time goes in v1:
time: 73 us; the launch traced here: 72.6 us
  waiting for transfers between devices  18 us (25%)
  blocking collectives  14.8 us (20%)
  starting transfers between devices  12.6 us (17%)
  Pallas kernels  11.9 us (16%)
  local copies, waits for them, and re-layouts  7.84 us (11%)
  other arithmetic  7.17 us (10%)
    all_to_all x1, waiting for transfers between devices, plane_shards(): received = lax.all_to_all(outgoing, grid, 0, 0, tiled=True)  15.4 us
    all_to_all x1, blocking collectives, plane_shards(): result = lax.all_to_all(result, grid, 0, 0, tiled=True)  14.8 us
    all_to_all x1, starting transfers between devices, plane_shards(): received = lax.all_to_all(outgoing, grid, 0, 0, tiled=True)  7.16 us
    pallas_call x2, Pallas kernels, correction_logs(): pl.pallas_call(correction_kernel, out_shape=jax.ShapeDtypeStruct(current....  7.03 us
    unnamed x29, local copies, waits for them, and re-layouts  6.68 us
    pallas_call x2, Pallas kernels, update(): pl.pallas_call(functools.partial(update_kernel, views), out_shape=(jax.Sh...  4.9 us
    ppermute x2, starting transfers between devices, plane_shards(): twin = lax.ppermute(current, 'gz', swap)  3.45 us
    ppermute x2, waiting for transfers between devices, plane_shards(): got = lax.ppermute(give, 'gz', swap)  2.52 us
  transfers between devices with their start and end apart: 7, of which 3 were waited for; matrix products, arithmetic and copies ran while one was open for 4% of the time, Pallas kernels for 10%

profile of v1, /device:TPU:0, one launch (start us, length us, event | category | flops | bytes accessed | tf_op | source)
XLA Modules:
  0.0 72.6 jit_solution(1728590527387711093)
XLA Ops:
  0.0 0.7 convert_bitcast_fusion
  0.7 0.7 convert.13
  1.6 1.0 %reduce-precision_convert_fusion = (bf16[8,64,128]{2,1,0:T(8,128)(2,1)S(1)}, bf16[8,64,128]{2,1,0:T(8,128)(2,1)S(1)}) fusion(f32[8,128,128]{2,1,0:T(8,128)} %param.5, s32[]{:T(128)S(6)} %select_n.39), kind=kLoop, calls=%fused_computation.5 | loop fusion | flops 262144 | bytes 524292 | tf_op jit(solution)/shard_map/convert_element_type | solution.py:301
  3.2 1.2 %collective-permute-done = bf16[4,272,128]{2,1,0:T(8,128)(2,1)S(1)} collective-permute-done((bf16[4,272,128]{2,1,0:T(8,128)(2,1)S(1)}, bf16[4,272,128]{2,1,0:T(8,128)(2,1)S(1)}, u32[]{:S(2)}, u32[]{:S(2)}) %collective-permute-start) | collective-permute-done | bytes 278560 | tf_op jit(solution)/shard_map/ppermute | solution.py:311
  6.3 0.6 slice_dynamic-update-slice_fusion.4
  8.8 0.6 slice_dynamic-update-slice_fusion
  9.5 7.2 %all-to-all-start = ((bf16[8,272,128]{2,1,0:T(8,128)(2,1)}), bf16[8,272,128]{2,1,0:T(8,128)(2,1)S(1)}, u32[]{:S(2)}, u32[]{:S(2)}) async-start(bf16[8,272,128]{2,1,0:T(8,128)(2,1)} %slice_dynamic-update-slice_fusion), calls=%async_computation | async-start | bytes 1114112 | tf_op jit(solution)/shard_map/all_to_all | solution.py:315
  16.7 15.4 %all-to-all-done = bf16[8,272,128]{2,1,0:T(8,128)(2,1)S(1)} async-done(((bf16[8,272,128]{2,1,0:T(8,128)(2,1)}), bf16[8,272,128]{2,1,0:T(8,128)(2,1)S(1)}, u32[]{:S(2)}, u32[]{:S(2)}) %all-to-all-start) | async-done | bytes 557088 | tf_op jit(solution)/shard_map/all_to_all | solution.py:315
  32.2 0.7 collective-permute-start.2
  32.9 2.1 %collective-permute-start.1 = (f32[512,128]{1,0:T(8,128)S(1)}, f32[512,128]{1,0:T(8,128)S(1)}, u32[]{:S(2)}, u32[]{:S(2)}) collective-permute-start(f32[512,128]{1,0:T(8,128)S(1)} %convert_add_fusion.current_ref), channel_id=1, source_target_pairs={{0,1},{1,0},{2,3},{3,2},{4,5},{5,4},{6,7},{7,6},{8,9},{9,8},{10,11... | collective-permute-start | bytes 786440 | tf_op jit(solution)/shard_map/ppermute | solution.py:341
  36.0 1.9 %multiply_reduce_fusion = bf16[2,4,2,128,128]{4,3,2,1,0:T(8,128)(2,1)} fusion(f32[128,128,9]{1,0,2:T(8,128)S(1)} %fusion, f32[2,1,2,9]{3,2,0,1:T(2,128)S(1)} %bitcast.64, f32[2,1,2,9]{3,2,0,1:T(2,128)S(1)} %bitcast.68, f32[2,1,2,9]{3,2,0,1:T(2,128)S(1)} %bitcast.67, f32[2,1,2,9]{3,2,0,1:T(2,128)S(1)} %bitcast.62), kind=kLoop, calls=%fused_computation | loop fusion | flops 4456880 | bytes 1114688 | tf_op jit(solution)/shard_map/vmap(vmap(vmap()))/reduce_sum | solution.py:41
  37.9 3.5 %correction.2.log_ref = f32[512,128]{1,0:T(8,128)} custom-call(s32[2,8]{1,0:T(2,128)} %slice_convert_fusion.1.offsets_ref, bf16[512,128]{1,0:T(8,128)(2,1)} %bitcast.53, bf16[4,2,272,128]{3,2,1,0:T(8,128)(2,1)} %bitcast.49, bf16[2,4,256,128]{3,2,1,0:T(8,128)(2,1)} %bitcast.51), custom_call_target="tpu_custom_call" | custom-call | flops 300000000 | bytes 1500000 | tf_op jit(solution)/shard_map/correction/pallas_call | solution.py:217
  41.4 0.7 copy-done.4
  42.2 2.5 %update.2 = (f32[512,128]{1,0:T(8,128)}, bf16[512,128]{1,0:T(8,128)(2,1)}) custom-call(s32[1]{0:T(128)} %bitcast.core_ref, f32[512,128]{1,0:T(8,128)} %copy-done.2, f32[512,128]{1,0:T(8,128)} %copy-done.5, f32[512,128]{1,0:T(8,128)} %copy-done.4, f32[512,128]{1,0:T(8,128)} %correction.2.log_ref), custom_call_target="tpu_custom_call" | custom-call | tf_op jit(solution)/shard_map/update/pallas_call | solution.py:269
  44.7 0.7 collective-permute-start.4
  45.4 1.3 %collective-permute-start.3 = (f32[512,128]{1,0:T(8,128)}, f32[512,128]{1,0:T(8,128)S(1)}, u32[]{:S(2)}, u32[]{:S(2)}) collective-permute-start(f32[512,128]{1,0:T(8,128)} %get-tuple-element.8.current_ref), channel_id=1, source_target_pairs={{0,1},{1,0},{2,3},{3,2},{4,5},{5,4},{6,7},{7,6},{8,9},{9,8},{10,11... | collective-permute-start | bytes 786440 | tf_op jit(solution)/shard_map/ppermute | solution.py:341
  46.7 3.5 %correction.3.log_ref = f32[512,128]{1,0:T(8,128)} custom-call(s32[2,8]{1,0:T(2,128)} %slice_convert_fusion.1.offsets_ref, bf16[512,128]{1,0:T(8,128)(2,1)} %get-tuple-element.9.current_ref, bf16[4,2,272,128]{3,2,1,0:T(8,128)(2,1)} %bitcast.50, bf16[2,4,256,128]{3,2,1,0:T(8,128)(2,1)} %bitcast.52), custom_call_target="tpu_custom_call" | custom-call | flops 300000000 | bytes 1500000 | tf_op jit(solution)/shard_map/correction/pallas_call | solution.py:217
  50.2 0.7 copy-done.6
  50.9 0.7 copy-done.7
  51.6 2.4 %update.3 = (f32[512,128]{1,0:T(8,128)}, bf16[512,128]{1,0:T(8,128)(2,1)}) custom-call(s32[1]{0:T(128)} %bitcast.core_ref, f32[512,128]{1,0:T(8,128)} %get-tuple-element.8.current_ref, f32[512,128]{1,0:T(8,128)} %copy-done.7, f32[512,128]{1,0:T(8,128)} %copy-done.6, f32[512,128]{1,0:T(8,128)} %correction.3.log_ref), custom_call_target="tpu_custom_call" | custom-call | tf_op jit(solution)/shard_map/update/pallas_call | solution.py:269
  54.1 1.0 %convert_element_type.69 = f16[512,128]{1,0:T(8,128)(2,1)S(1)} convert(f32[512,128]{1,0:T(8,128)} %get-tuple-element.10) | non-fusion elementwise | flops 65536 | bytes 393216 | tf_op jit(solution)/shard_map/convert_element_type | solution.py:345
  55.1 14.8 %all_to_all.10 = f16[8,128,128]{2,1,0:T(8,128)(2,1)S(1)} all-to-all(f16[8,128,128]{2,1,0:T(8,128)(2,1)S(1)} %bitcast.54), channel_id=1, replica_groups=mesh['groups'=2,'tiles'=4,'views'=2,'gz'=2] {'tiles','views'}, dimensions={0} | all-to-all | bytes 524288 | tf_op jit(solution)/shard_map/all_to_all | solution.py:347
  70.2 1.3 %collective-permute-done.5 = f16[4,128,128]{2,1,0:T(8,128)(2,1)S(1)} collective-permute-done((f16[4,128,128]{2,1,0:T(8,128)(2,1)S(1)}, f16[4,128,128]{2,1,0:T(8,128)(2,1)S(1)}, u32[]{:S(2)}, u32[]{:S(2)}) %collective-permute-start.5) | collective-permute-done | bytes 131104 | tf_op jit(solution)/shard_map/ppermute | solution.py:352
  71.7 0.8 %bitcast_convert_fusion = f32[8,128,128]{2,1,0:T(8,128)} fusion(f16[4,2,128,128]{3,2,1,0:T(8,128)(2,1)S(1)} %pad_maximum_fusion.1), kind=kLoop, calls=%fused_computation.11 | loop fusion | flops 131072 | bytes 786432 | tf_op jit(solution)/shard_map/convert_element_type | solution.py:355
  (52 shorter events, 6.2 us)
Async XLA Ops:
  0.0 2.6 %copy-start.3 = (bf16[1,1,8,128,128]{4,3,2,1,0:T(8,128)(2,1)S(1)}, bf16[1,1,8,128,128]{4,3,2,1,0:T(8,128)(2,1)}, u32[]{:S(2)}) copy-start(bf16[1,1,8,128,128]{4,3,2,1,0:T(8,128)(2,1)} %param.4) | copy-start | bytes 786436
  2.7 1.7 %collective-permute-start = (bf16[4,272,128]{2,1,0:T(8,128)(2,1)S(1)}, bf16[4,272,128]{2,1,0:T(8,128)(2,1)S(1)}, u32[]{:S(2)}, u32[]{:S(2)}) collective-permute-start(bf16[4,272,128]{2,1,0:T(8,128)(2,1)S(1)} %dynamic-slice_bitcast_fusion), channel_id=1, source_target_pairs={{0,1},{1,0},{2,3},{3,2},{4,5},{5,4},{6,7},{7,6},{8,9},{9,8},{10,11... | collective-permute-start | bytes 835592 | tf_op jit(solution)/shard_map/ppermute | solution.py:311
  9.5 22.7 %all-to-all-start = ((bf16[8,272,128]{2,1,0:T(8,128)(2,1)}), bf16[8,272,128]{2,1,0:T(8,128)(2,1)S(1)}, u32[]{:S(2)}, u32[]{:S(2)}) async-start(bf16[8,272,128]{2,1,0:T(8,128)(2,1)} %slice_dynamic-update-slice_fusion), calls=%async_computation | async-start | bytes 1114112 | tf_op jit(solution)/shard_map/all_to_all | solution.py:315
  32.1 5.8 %copy-start = (bf16[8,272,128]{2,1,0:T(8,128)(2,1)}, bf16[8,272,128]{2,1,0:T(8,128)(2,1)S(1)}, u32[]{:S(2)}) copy-start(bf16[8,272,128]{2,1,0:T(8,128)(2,1)S(1)} %all-to-all-done) | copy-start | bytes 1671172
  32.2 5.7 %copy-start.1 = (bf16[4,2,64,128]{3,2,1,0:T(8,128)(2,1)}, bf16[4,2,64,128]{3,2,1,0:T(8,128)(2,1)S(1)}, u32[]{:S(2)}) copy-start(bf16[4,2,64,128]{3,2,1,0:T(8,128)(2,1)S(1)} %get-tuple-element.13) | copy-start | bytes 393220
  32.2 9.2 %copy-start.2 = (f32[512,128]{1,0:T(8,128)}, f32[512,128]{1,0:T(8,128)S(1)}, u32[]{:S(2)}) copy-start(f32[512,128]{1,0:T(8,128)S(1)} %convert_add_fusion.current_ref) | copy-start | bytes 786436
  32.2 9.2 %collective-permute-start.2 = (f32[512,128]{1,0:T(8,128)S(1)}, f32[512,128]{1,0:T(8,128)S(1)}, u32[]{:S(2)}, u32[]{:S(2)}) collective-permute-start(f32[512,128]{1,0:T(8,128)S(1)} %convert_add_fusion.current_ref), channel_id=1, source_target_pairs={{1,4},{4,1},{5,8},{8,5},{9,12},{12,9},{13,14},{14,13},{15,10},{10,... | collective-permute-start | bytes 786440 | tf_op jit(solution)/shard_map/ppermute | solution.py:340
  32.9 8.5 %collective-permute-start.1 = (f32[512,128]{1,0:T(8,128)S(1)}, f32[512,128]{1,0:T(8,128)S(1)}, u32[]{:S(2)}, u32[]{:S(2)}) collective-permute-start(f32[512,128]{1,0:T(8,128)S(1)} %convert_add_fusion.current_ref), channel_id=1, source_target_pairs={{0,1},{1,0},{2,3},{3,2},{4,5},{5,4},{6,7},{7,6},{8,9},{9,8},{10,11... | collective-permute-start | bytes 786440 | tf_op jit(solution)/shard_map/ppermute | solution.py:341
  41.4 0.7 copy-start.4
  41.4 0.8 %copy-start.5 = (f32[512,128]{1,0:T(8,128)}, f32[512,128]{1,0:T(8,128)S(1)}, u32[]{:S(2)}) copy-start(f32[512,128]{1,0:T(8,128)S(1)} %collective-permute-done.1.twin_ref) | copy-start | bytes 786436
  44.7 5.5 %collective-permute-start.4 = (f32[512,128]{1,0:T(8,128)}, f32[512,128]{1,0:T(8,128)S(1)}, u32[]{:S(2)}, u32[]{:S(2)}) collective-permute-start(f32[512,128]{1,0:T(8,128)} %get-tuple-element.8.current_ref), channel_id=1, source_target_pairs={{1,4},{4,1},{5,8},{8,5},{9,12},{12,9},{13,14},{14,13},{15,10},{10,... | collective-permute-start | bytes 786440 | tf_op jit(solution)/shard_map/ppermute | solution.py:340
  45.4 4.9 %collective-permute-start.3 = (f32[512,128]{1,0:T(8,128)}, f32[512,128]{1,0:T(8,128)S(1)}, u32[]{:S(2)}, u32[]{:S(2)}) collective-permute-start(f32[512,128]{1,0:T(8,128)} %get-tuple-element.8.current_ref), channel_id=1, source_target_pairs={{0,1},{1,0},{2,3},{3,2},{4,5},{5,4},{6,7},{7,6},{8,9},{9,8},{10,11... | collective-permute-start | bytes 786440 | tf_op jit(solution)/shard_map/ppermute | solution.py:341
  50.2 0.7 copy-start.6
  50.9 0.7 copy-start.7
  70.1 1.4 %collective-permute-start.5 = (f16[4,128,128]{2,1,0:T(8,128)(2,1)S(1)}, f16[4,128,128]{2,1,0:T(8,128)(2,1)S(1)}, u32[]{:S(2)}, u32[]{:S(2)}) collective-permute-start(f16[4,128,128]{2,1,0:T(8,128)(2,1)S(1)} %dynamic-slice_bitcast_fusion.1), channel_id=1, source_target_pairs={{0,1},{1,0},{2,3},{3,2},{4,5},{5,4},{6,7},{7,6},{8,9},{9,8},{10,11... | collective-permute-start | bytes 393224 | tf_op jit(solution)/shard_map/ppermute | solution.py:352
